TPU v7x, 256 devices: a whole 4x4x8 slice. The times are simulated.
256 devices in a mesh: row: 8 (over z_hi, x), col: 32 (over z_lo, y, core).
Axes of the slice: x: 4, y: 4, z: 8 (z_hi: 2, z_lo: 4; z = z_hi * 4 + z_lo), core: 2. Of those that a mesh axis runs over, the one named last changes fastest.
Arguments:
- contexts: bfloat16 [32768, 128], P(('row', 'col')), may hold values from -8 to 8
- logged_actions: int32 [32768], P(('row', 'col')), may hold values from 0 to 131041
- policy_actions: int32 [32768, 8], P(('row', 'col')), may hold values from 0 to 131041
- rewards: float32 [32768], P(('row', 'col')), may hold values from 0.2 to 2
Outputs:
- weights: float32 [32768, 8], P(('row', 'col'))
- residual: float32 [32768, 8], P(('row', 'col'))
- values: float32 [8], replicated
All inputs are finite; a program needn't handle non-finite values.
Results may differ from a plain program's by a relative error of at most 0.0056.
Values may be sent and summed in bfloat16 or wider, within the bound.
No kernel may reach another device: no remote copies, remote signals or barrier semaphores. Data moves between devices by JAX's collectives and lax.ppermute only.
A program may use at most 64 MiB of HBM per device.

v0:
```python
import math
import jax
import jax.numpy as jnp
from jax import lax
from jax.sharding import PartitionSpec as P

NPOL = 8
NACT = 16
CATALOG = 131042
ridge = 0.1
group_size = 16
stride_base = 1009
phase_step = 0.37
two_pi = 2.0 * math.pi


def action_features(chosen, width):
    levels = jnp.arange(width, dtype=jnp.int32)
    multipliers = 1 + stride_base * levels
    turned = chosen[..., None] * multipliers % CATALOG
    angles = turned.astype(jnp.float32) * (two_pi / CATALOG) + phase_step * levels.astype(
        jnp.float32
    )
    wave_terms = math.sqrt(2.0 / width) * jnp.cos(angles)
    constant_term = jnp.full(wave_terms.shape, 1.0 / math.sqrt(width), jnp.float32)
    return jnp.where(levels == 0, constant_term, wave_terms).astype(jnp.bfloat16)


def select_actions(products, onehot):
    shaped = products.reshape(
        products.shape[:-1] + (products.shape[-1] // onehot.shape[-1], onehot.shape[-1])
    )
    return jnp.sum(shaped * jnp.expand_dims(onehot.astype(jnp.float32), -2), axis=-1)


def kernel_tiles(left_tiles, right_tiles, left_squares, right_squares):
    inner = jnp.einsum("grd,gsd->grs", left_tiles, right_tiles, preferred_element_type=jnp.float32)
    expo = (2.0 * inner - left_squares[:, :, None] - right_squares[:, None, :]) / left_tiles.shape[
        -1
    ]
    return jnp.exp(expo).astype(jnp.bfloat16)


def tile_terms(kernel, left_matrix, right_matrix, left_onehot, right_onehot):
    toward_left = jnp.einsum(
        "grs,gsm->grm", kernel, right_matrix, preferred_element_type=jnp.float32
    )
    toward_right = jnp.einsum(
        "grs,grm->gsm", kernel, left_matrix, preferred_element_type=jnp.float32
    )
    return (select_actions(toward_left, left_onehot), select_actions(toward_right, right_onehot))


def listed_pass(
    left_ctx,
    left_squares,
    left_matrix,
    left_onehot,
    right_ctx,
    right_squares,
    right_matrix,
    right_onehot,
    placed,
    diagonal,
):
    left_count = left_ctx.shape[0]
    tile_rows = left_ctx.shape[1]
    right_count = right_ctx.shape[0]
    policies = left_matrix.shape[-1] // left_onehot.shape[-1]
    flat_placed = placed.reshape(-1)
    flat_diagonal = diagonal.reshape(-1)
    plan = jnp.argsort(1 - flat_placed, stable=True)
    active_count = jnp.sum(flat_placed)
    rounds = (active_count + group_size - 1) // group_size

    def advance(round_index, carried):
        row_sums, column_sums = carried
        picked = lax.dynamic_slice_in_dim(plan, round_index * group_size, group_size)
        left_pick = picked // right_count
        right_pick = picked % right_count
        live_flags = jnp.take(flat_placed, picked).astype(jnp.float32)
        mirror_flags = live_flags * (1 - jnp.take(flat_diagonal, picked)).astype(jnp.float32)
        kernel = kernel_tiles(
            left_ctx[left_pick],
            right_ctx[right_pick],
            left_squares[left_pick],
            right_squares[right_pick],
        )
        toward_left, toward_right = tile_terms(
            kernel,
            left_matrix[left_pick],
            right_matrix[right_pick],
            left_onehot[left_pick],
            right_onehot[right_pick],
        )
        row_sums = row_sums.at[left_pick].add(toward_left * live_flags[:, None, None])
        column_sums = column_sums.at[right_pick].add(toward_right * mirror_flags[:, None, None])
        return (row_sums, column_sums)

    start_rows = jnp.zeros((left_count, tile_rows, policies), jnp.float32)
    start_columns = jnp.zeros((right_count, tile_rows, policies), jnp.float32)
    return lax.fori_loop(0, rounds, advance, (start_rows, start_columns))


def on_device(contexts, logged_actions, policy_actions, rewards):
    tile_rows, feature_count = contexts.shape
    left_count = lax.axis_size("col")
    right_count = lax.axis_size("row")
    factor = NACT / (tile_rows * left_count * right_count)
    own_column = lax.axis_index("col")
    own_row = lax.axis_index("row")
    left_ids = jnp.arange(left_count, dtype=jnp.int32)[:, None]
    right_ids = jnp.arange(right_count, dtype=jnp.int32)[None, :]
    first_owner = own_row * left_count + left_ids
    second_owner = right_ids * left_count + own_column
    parity = (first_owner + second_owner) % 2
    placed = jnp.where(
        first_owner == second_owner, 1, jnp.where(first_owner < second_owner, parity, 1 - parity)
    )
    diagonal = ((left_ids == own_column) & (right_ids == own_row)).astype(jnp.int32)
    left_logged, left_policy = (
        lax.all_gather(logged_actions, "col", axis=0, tiled=True),
        lax.all_gather(policy_actions, "col", axis=0, tiled=True),
    )
    right_logged, right_policy = (
        lax.all_gather(logged_actions, "row", axis=0, tiled=True),
        lax.all_gather(policy_actions, "row", axis=0, tiled=True),
    )
    left_onehot = action_features(left_logged, NACT).reshape(left_count, tile_rows, NACT)
    right_onehot = action_features(right_logged, NACT).reshape(right_count, tile_rows, NACT)
    left_first = action_features(left_policy, NACT).reshape(left_count, tile_rows, NPOL * NACT)
    right_first = action_features(right_policy, NACT).reshape(right_count, tile_rows, NPOL * NACT)
    right_ctx = lax.all_gather(contexts, "row", axis=0, tiled=True).reshape(
        right_count, tile_rows, feature_count
    )
    right_squares = jnp.sum(right_ctx.astype(jnp.float32) ** 2, axis=2)
    left_ctx = lax.all_gather(contexts, "col", axis=0, tiled=True).reshape(
        left_count, tile_rows, feature_count
    )
    left_squares = jnp.sum(left_ctx.astype(jnp.float32) ** 2, axis=2)

    def sweep(left_matrix, right_matrix):
        return listed_pass(
            left_ctx,
            left_squares,
            left_matrix,
            left_onehot,
            right_ctx,
            right_squares,
            right_matrix,
            right_onehot,
            placed,
            diagonal,
        )

    def reduce_terms(toward_left, toward_right):
        mine_left = lax.psum_scatter(toward_left, "col", scatter_dimension=0, tiled=True)
        mine_right = lax.psum_scatter(toward_right, "row", scatter_dimension=0, tiled=True)
        return factor * (mine_left[0] + mine_right[0])

    first_left, first_right = sweep(left_first, right_first)
    right_side = reduce_terms(first_left, first_right)
    right_low = right_side.astype(jnp.bfloat16)
    left_rhs = lax.all_gather(right_low, "col", axis=0, tiled=True).reshape(
        left_count, tile_rows, NPOL
    )
    right_rhs = lax.all_gather(right_low, "row", axis=0, tiled=True).reshape(
        right_count, tile_rows, NPOL
    )
    left_second = (left_onehot[:, :, None, :] * left_rhs[:, :, :, None]).reshape(
        left_count, tile_rows, NPOL * NACT
    )
    right_second = (right_onehot[:, :, None, :] * right_rhs[:, :, :, None]).reshape(
        right_count, tile_rows, NPOL * NACT
    )
    second_left, second_right = sweep(left_second, right_second)
    image = reduce_terms(second_left, second_right) + ridge * right_side
    norm_sums, curvature, reward_sums = lax.psum(
        (
            jnp.sum(right_side * right_side, axis=0),
            jnp.sum(right_side * image, axis=0),
            jnp.sum(rewards[:, None] * right_side, axis=0),
        ),
        ("row", "col"),
    )
    alpha = norm_sums / curvature
    weights = alpha[None, :] * right_side
    residual = right_side - alpha[None, :] * image
    values = alpha * reward_sums / (tile_rows * left_count * right_count)
    return (weights, residual, values)


def solution(mesh):
    placed = (
        P(("row", "col"), None),
        P(("row", "col")),
        P(("row", "col"), None),
        P(("row", "col")),
    )
    return jax.shard_map(
        on_device,
        mesh=mesh,
        in_specs=placed,
        out_specs=(P(("row", "col"), None), P(("row", "col"), None), P()),
        check_vma=False,
    )
```

profile of v0, /device:TPU:1, one launch (start us, length us, event | category | flops | bytes accessed | tf_op | source)
XLA Modules:
  0.0 1289.7 jit_solution(7908967299347687956)
XLA Ops:
  11.6 3.2 sort.19
  14.8 29.4 %all-gather.1 = s32[8,1,128]{2,1,0:T(1,128)S(1)} all-gather(s32[1,1,128]{2,1,0:T(1,128)} %bitcast.113), channel_id=1, replica_groups=mesh['row'=8,'col'=32] {'row'}, dimensions={0}, use_global_device_ids=true | all-gather | bytes 4608 | tf_op jit(solution)/shard_map/all_gather | solution.py:126
  44.2 46.1 %all-gather = s32[32,1,128]{2,1,0:T(1,128)S(1)} all-gather(s32[1,1,128]{2,1,0:T(1,128)} %bitcast.114), channel_id=1, replica_groups=mesh['row'=8,'col'=32] {'col'}, dimensions={0}, use_global_device_ids=true | all-gather | bytes 16896 | tf_op jit(solution)/shard_map/all_gather | solution.py:122
  90.3 37.4 %all_gather.26 = s32[1024,8]{0,1:T(8,128)S(1)} all-gather(s32[128,8]{0,1:T(8,128)} %param.12), channel_id=1, replica_groups=mesh['row'=8,'col'=32] {'row'}, dimensions={0}, use_global_device_ids=true | all-gather | bytes 36864 | tf_op jit(solution)/shard_map/all_gather | solution.py:127
  127.8 44.6 %all_gather.28 = s32[4096,8]{0,1:T(8,128)S(1)} all-gather(s32[128,8]{0,1:T(8,128)} %param.12), channel_id=1, replica_groups=mesh['row'=8,'col'=32] {'col'}, dimensions={0}, use_global_device_ids=true | all-gather | bytes 135168 | tf_op jit(solution)/shard_map/all_gather | solution.py:123
  173.5 37.9 %all_gather.25 = bf16[1024,128]{1,0:T(8,128)(2,1)S(1)} all-gather(bf16[128,128]{1,0:T(8,128)(2,1)} %param.10), channel_id=1, replica_groups=mesh['row'=8,'col'=32] {'row'}, dimensions={0}, use_global_device_ids=true | all-gather | bytes 294912 | tf_op jit(solution)/shard_map/all_gather | solution.py:133
  212.7 1.8 multiply_reduce_fusion.4
  214.6 266.5 %while.32 = (s32[]{:T(128)}, f32[32,128,8]{1,2,0:T(8,128)S(1)}, f32[8,128,8]{1,2,0:T(8,128)S(1)}, s32[]{:T(128)}, s32[256]{0:T(256)}, /*index=5*/bf16[32,128,128...) while((s32[]{:T(128)}, f32[32,128,8]{1,2,0:T(8,128)S(1)}, ...), condition=%wide.region_9.11_spmd.clone.clone, body=%wide.region_4.10_spmd.clone.clone.sunk | while | flops 213377504 | bytes 27038416 | solution.py:102
  217.6 1.9 gather_fusion.1
  222.1 1.9 copy.56
  224.0 9.3 fusion.174
  238.1 2.1 fusion.171
  247.1 1.9 gather_fusion.1
  251.6 1.9 copy.56
  253.6 9.3 fusion.174
  267.7 2.1 fusion.171
  276.7 1.9 gather_fusion.1
  281.2 1.9 copy.56
  283.2 9.3 fusion.174
  297.3 2.1 fusion.171
  306.3 1.9 gather_fusion.1
  310.8 1.9 copy.56
  312.8 9.3 fusion.174
  326.9 2.1 fusion.171
  335.9 1.9 gather_fusion.1
  340.4 1.9 copy.56
  342.3 9.3 fusion.174
  356.5 2.1 fusion.171
  365.5 1.9 gather_fusion.1
  370.0 1.9 copy.56
  371.9 9.3 fusion.174
  386.1 2.1 fusion.171
  395.1 1.9 gather_fusion.1
  399.6 1.9 copy.56
  401.5 9.3 fusion.174
  415.7 2.1 fusion.171
  424.7 1.9 gather_fusion.1
  429.2 1.9 copy.56
  431.1 9.3 fusion.174
  445.3 2.1 fusion.171
  454.3 1.9 gather_fusion.1
  458.8 1.9 copy.56
  460.7 9.3 fusion.174
  474.8 2.1 fusion.171
  484.7 39.5 %all-reduce.1 = f32[8,128,8]{1,2,0:T(8,128)S(1)} all-reduce(f32[8,128,8]{1,2,0:T(8,128)S(1)} %get-tuple-element.391), channel_id=3, replica_groups=mesh['row'=8,'col'=32] {'row'}, use_global_device_ids=true, to_apply=%region_11.13.clone | all-reduce | flops 8192 | bytes 65536
  524.3 203.3 %all-reduce.8.cloned.1.call-done = f32[32,128,8]{1,2,0:T(8,128)} async-done(((f32[32,128,8]{1,2,0:T(8,128)}), f32[32,128,8]{1,2,0:T(8,128)}) %all-reduce.8.cloned.1.call-update) | async-done | bytes 131088
  727.5 2.5 multiply_convert_fusion
  730.1 39.7 %all_gather.31 = bf16[4096,8]{0,1:T(8,128)(2,1)S(1)} all-gather(bf16[128,8]{0,1:T(8,128)(2,1)S(1)} %get-tuple-element.780), channel_id=1, replica_groups=mesh['row'=8,'col'=32] {'col'}, dimensions={0}, use_global_device_ids=true | all-gather | bytes 67584 | tf_op jit(solution)/shard_map/all_gather | solution.py:164
  769.7 35.1 %all_gather.30 = bf16[1024,8]{0,1:T(8,128)(2,1)S(1)} all-gather(bf16[128,8]{0,1:T(8,128)(2,1)S(1)} %get-tuple-element.780), channel_id=1, replica_groups=mesh['row'=8,'col'=32] {'row'}, dimensions={0}, use_global_device_ids=true | all-gather | bytes 18432 | tf_op jit(solution)/shard_map/all_gather | solution.py:167
  804.8 144.6 %while.33 = (s32[]{:T(128)}, f32[32,128,8]{1,2,0:T(8,128)S(1)}, f32[8,128,8]{1,2,0:T(8,128)S(1)}, s32[]{:T(128)}, s32[256]{0:T(256)}, /*index=5*/bf16[32,128,128...) while((s32[]{:T(128)}, f32[32,128,8]{1,2,0:T(8,128)S(1)}, ...), condition=%wide.region_19.21_spmd.clone.clone, body=%wide.region_14.20_spmd.clone.clone.sunk | while | flops 205513184 | bytes 14005563 | solution.py:102
  807.8 1.9 gather_fusion.11
  823.9 1.9 gather_fusion.11
  839.9 1.9 gather_fusion.11
  855.9 1.9 gather_fusion.11
  872.0 1.9 gather_fusion.11
  888.0 1.9 gather_fusion.11
  904.1 1.9 gather_fusion.11
  920.1 1.9 gather_fusion.11
  936.1 1.9 gather_fusion.11
  950.7 45.4 %all-reduce.3 = f32[8,128,8]{1,2,0:T(8,128)S(1)} all-reduce(f32[8,128,8]{1,2,0:T(8,128)S(1)} %get-tuple-element.393), channel_id=5, replica_groups=mesh['row'=8,'col'=32] {'row'}, use_global_device_ids=true, to_apply=%region_21.23.clone | all-reduce | flops 8192 | bytes 65536
  996.1 204.5 %all-reduce.10.cloned.1.call-done = f32[32,128,8]{1,2,0:T(8,128)} async-done(((f32[32,128,8]{1,2,0:T(8,128)}), f32[32,128,8]{1,2,0:T(8,128)}) %all-reduce.10.cloned.1.call-update) | async-done | bytes 131088
  1200.6 2.1 multiply_reduce_fusion.6
  1202.7 77.4 %all-reduce.4 = (f32[8]{0:T(128)S(1)}, f32[8]{0:T(128)S(1)}, f32[8]{0:T(128)S(1)}) all-reduce(f32[8]{0:T(128)S(1)} %get-tuple-element.680, f32[8]{0:T(128)S(1)} %get-tuple-element.679, f32[8]{0:T(128)S(1)} %get-tuple-element.678), channel_id=1, replica_groups=mesh['row'=8,'col'=32] {'row','col'}, use_global_device_ids=true, to_apply=%region_13.15 | all-reduce | flops 24 | bytes 192 | tf_op jit(solution)/shard_map/psum | solution.py:178
  1280.6 2.6 multiply_subtract_fusion
  (880 shorter events, 264.3 us)
Async XLA Ops:
  7.2 205.5 %all-gather.4.cloned.1.call-start = ((), (), s32[]{:S(2)}) async-start(), calls=%async_computation | async-start | bytes 1081344 | tf_op jit(solution)/shard_map/all_gather | solution.py:137
  7.9 719.6 %all-reduce.8.cloned.1.call-start = ((), (), s32[]{:S(2)}) async-start(), calls=%async_computation.1 | async-start | bytes 262144
  217.5 1.9 copy-start.2
  224.0 10.3 copy-start.6
  224.0 10.4 copy-start.8
  237.5 0.7 copy-start.10
  240.2 3.0 copy-start.3
  247.1 1.9 copy-start.2
  253.6 10.3 copy-start.6
  253.6 10.4 copy-start.8
  267.1 0.7 copy-start.10
  269.8 3.0 copy-start.3
  276.7 1.9 copy-start.2
  283.2 10.3 copy-start.6
  283.2 10.4 copy-start.8
  296.7 0.7 copy-start.10
  299.4 3.0 copy-start.3
  306.3 1.9 copy-start.2
  312.8 10.3 copy-start.6
  312.8 10.4 copy-start.8
  326.2 0.7 copy-start.10
  329.0 3.0 copy-start.3
  335.9 1.9 copy-start.2
  342.3 10.3 copy-start.6
  342.3 10.4 copy-start.8
  355.8 0.7 copy-start.10
  358.6 3.0 copy-start.3
  365.5 1.9 copy-start.2
  371.9 10.3 copy-start.6
  371.9 10.4 copy-start.8
  385.4 0.7 copy-start.10
  388.2 3.0 copy-start.3
  395.1 1.9 copy-start.2
  401.5 10.3 copy-start.6
  401.5 10.4 copy-start.8
  417.7 3.0 copy-start.3
  424.7 1.9 copy-start.2
  431.1 10.3 copy-start.6
  431.1 10.4 copy-start.8
  444.6 0.7 copy-start.10
  447.3 3.0 copy-start.3
  454.2 1.9 copy-start.2
  460.7 10.3 copy-start.6
  460.7 10.4 copy-start.8
  476.9 3.0 copy-start.3
  481.7 718.9 %all-reduce.10.cloned.1.call-start = ((), (), s32[]{:S(2)}) async-start(), calls=%async_computation.2 | async-start | bytes 262144
  811.9 1.8 copy-start.7
  811.9 1.8 copy-start.9
  827.9 1.8 copy-start.7
  827.9 1.8 copy-start.9
  843.9 1.8 copy-start.7
  843.9 1.8 copy-start.9
  860.0 1.8 copy-start.7
  860.0 1.8 copy-start.9
  876.0 1.8 copy-start.7
  876.0 1.8 copy-start.9
  892.0 1.8 copy-start.7
  892.1 1.8 copy-start.9
  908.1 1.8 copy-start.7
  908.1 1.8 copy-start.9
  924.1 1.8 copy-start.7
  924.1 1.8 copy-start.9
  940.2 1.8 copy-start.7
  940.2 1.8 copy-start.9
  (22 other events, 13.3 us)
Sparse Core Ops, SparseCore 0:
  9.9 63.0 all-gather.3
  481.9 245.6 all-reduce.7
  950.2 250.3 all-reduce.9
where the time goes:
time: 1290 us
  blocking collectives  432 us (33%)
  waiting for transfers between devices  409 us (32%)
  other arithmetic  221 us (17%)
  local copies, waits for them, and re-layouts  183 us (14%)
  matrix products  25.4 us (2%)
  between operations  14.6 us (1%)
    unnamed x5, waiting for transfers between devices  408 us
    convert_element_type x56, other arithmetic, action_features(): jnp.where(levels == 0, constant_term, wave_terms).astype(jnp.bfloat16)  130 us
    unnamed x2, blocking collectives  84.9 us
    psum x1, blocking collectives, on_device(): lax.psum((jnp.sum(right_side * right_side, axis=0), jnp.sum(right_side *...  77.4 us
    all_gather x1, blocking collectives, on_device(): lax.all_gather(logged_actions, 'col', axis=0, tiled=True)  46.1 us
    all_gather x1, blocking collectives, on_device(): lax.all_gather(policy_actions, 'col', axis=0, tiled=True)  44.6 us
    all_gather x1, blocking collectives, on_device(): lax.all_gather(right_low, 'col', axis=0, tiled=True)  39.7 us
    all_gather x1, blocking collectives, on_device(): lax.all_gather(contexts, 'row', axis=0, tiled=True)  37.9 us
  transfers between devices with their start and end apart: 3, of which 2 were waited for; matrix products, arithmetic and copies ran while one was open for 1% of the time, Pallas kernels for 0%

commit v1 on v0

--- a/solution.py
+++ b/solution.py
@@ -123,7 +123,9 @@
         lax.all_gather(policy_actions, "col", axis=0, tiled=True),
     )
     right_logged, right_policy = (
-        lax.all_gather(logged_actions, "row", axis=0, tiled=True),
+        jnp.concatenate(
+            lax.all_to_all(jnp.stack([logged_actions] * lax.axis_size("row")), "row", 0, 0), axis=0
+        ),
         lax.all_gather(policy_actions, "row", axis=0, tiled=True),
     )
     left_onehot = action_features(left_logged, NACT).reshape(left_count, tile_rows, NACT)

time: 1290 us -> 1280 us (level)
  blocking collectives: 432 us -> 407 us
    all_gather x1 -> x0, blocking collectives: 29.4 us -> none  [on_device(): lax.all_gather(logged_actions, 'row', axis=0, tiled=True)]
  transfers between devices with their start and end apart: 3 -> 4, of which waited for: 2 -> 2; matrix products, arithmetic and copies ran while one was open for 1% -> 1% of each run, Pallas kernels for 0% -> 0%
where the time goes in v1:
time: 1280 us
  waiting for transfers between devices  409 us (32%)
  blocking collectives  407 us (32%)
  other arithmetic  221 us (17%)
  local copies, waits for them, and re-layouts  184 us (14%)
  matrix products  25.5 us (2%)
  between operations  14.6 us (1%)
    unnamed x5, waiting for transfers between devices  409 us
    convert_element_type x56, other arithmetic, action_features(): jnp.where(levels == 0, constant_term, wave_terms).astype(jnp.bfloat16)  130 us
    unnamed x2, blocking collectives  91.4 us
    psum x1, blocking collectives, on_device(): lax.psum((jnp.sum(right_side * right_side, axis=0), jnp.sum(right_side *...  77.3 us
    all_gather x1, blocking collectives, on_device(): lax.all_gather(policy_actions, 'col', axis=0, tiled=True)  44.6 us
    all_gather x1, blocking collectives, on_device(): lax.all_gather(logged_actions, 'col', axis=0, tiled=True)  42.6 us
    all_gather x1, blocking collectives, on_device(): lax.all_gather(right_low, 'col', axis=0, tiled=True)  39.7 us
    all_gather x1, blocking collectives, on_device(): lax.all_gather(contexts, 'row', axis=0, tiled=True)  38.2 us
  transfers between devices with their start and end apart: 4, of which 2 were waited for; matrix products, arithmetic and copies ran while one was open for 1% of the time, Pallas kernels for 0%

profile of v1, /device:TPU:1, one launch (start us, length us, event | category | flops | bytes accessed | tf_op | source)
XLA Modules:
  0.0 1277.8 jit_solution(14978036537835507517)
XLA Ops:
  9.2 11.5 all-to-all-start
  27.0 3.2 sort.19
  30.2 42.6 %all-gather = s32[32,1,128]{2,1,0:T(1,128)S(1)} all-gather(s32[1,1,128]{2,1,0:T(1,128)} %bitcast.113), channel_id=1, replica_groups=mesh['row'=8,'col'=32] {'col'}, dimensions={0}, use_global_device_ids=true | all-gather | bytes 16896 | tf_op jit(solution)/shard_map/all_gather | solution.py:122
  72.8 38.2 %all_gather.23 = s32[1024,8]{0,1:T(8,128)S(1)} all-gather(s32[128,8]{0,1:T(8,128)} %param.12), channel_id=1, replica_groups=mesh['row'=8,'col'=32] {'row'}, dimensions={0}, use_global_device_ids=true | all-gather | bytes 36864 | tf_op jit(solution)/shard_map/all_gather | solution.py:129
  111.1 44.6 %all_gather.25 = s32[4096,8]{0,1:T(8,128)S(1)} all-gather(s32[128,8]{0,1:T(8,128)} %param.12), channel_id=1, replica_groups=mesh['row'=8,'col'=32] {'col'}, dimensions={0}, use_global_device_ids=true | all-gather | bytes 135168 | tf_op jit(solution)/shard_map/all_gather | solution.py:123
  156.7 38.2 %all_gather.22 = bf16[1024,128]{1,0:T(8,128)(2,1)S(1)} all-gather(bf16[128,128]{1,0:T(8,128)(2,1)} %param.10), channel_id=1, replica_groups=mesh['row'=8,'col'=32] {'row'}, dimensions={0}, use_global_device_ids=true | all-gather | bytes 294912 | tf_op jit(solution)/shard_map/all_gather | solution.py:135
  196.3 1.8 multiply_reduce_fusion.4
  198.1 266.5 %while.32 = (s32[]{:T(128)}, f32[32,128,8]{1,2,0:T(8,128)S(1)}, f32[8,128,8]{1,2,0:T(8,128)S(1)}, s32[]{:T(128)}, s32[256]{0:T(256)}, /*index=5*/bf16[32,128,128...) while((s32[]{:T(128)}, f32[32,128,8]{1,2,0:T(8,128)S(1)}, ...), condition=%wide.region_9.11_spmd.clone.clone, body=%wide.region_4.10_spmd.clone.clone.sunk | while | flops 213377504 | bytes 27038416 | solution.py:102
  201.1 1.9 gather_fusion.1
  205.6 1.9 copy.56
  207.5 9.3 fusion.174
  221.7 2.1 fusion.171
  230.7 1.9 gather_fusion.1
  235.2 1.9 copy.56
  237.1 9.3 fusion.174
  251.3 2.1 fusion.171
  260.3 1.9 gather_fusion.1
  264.8 1.9 copy.56
  266.7 9.3 fusion.174
  280.9 2.1 fusion.171
  289.9 1.9 gather_fusion.1
  294.4 1.9 copy.56
  296.3 9.3 fusion.174
  310.5 2.1 fusion.171
  319.5 1.9 gather_fusion.1
  324.0 1.9 copy.56
  325.9 9.3 fusion.174
  340.1 2.1 fusion.171
  349.1 1.9 gather_fusion.1
  353.6 1.9 copy.56
  355.5 9.3 fusion.174
  369.7 2.1 fusion.171
  378.6 1.9 gather_fusion.1
  383.1 1.9 copy.56
  385.1 9.3 fusion.174
  399.3 2.1 fusion.171
  408.2 1.9 gather_fusion.1
  412.7 1.9 copy.56
  414.7 9.3 fusion.174
  428.8 2.1 fusion.171
  437.8 1.9 gather_fusion.1
  442.3 1.9 copy.56
  444.3 9.3 fusion.174
  458.4 2.1 fusion.171
  465.7 45.9 %all-reduce.1 = f32[8,128,8]{1,2,0:T(8,128)S(1)} all-reduce(f32[8,128,8]{1,2,0:T(8,128)S(1)} %get-tuple-element.391), channel_id=3, replica_groups=mesh['row'=8,'col'=32] {'row'}, use_global_device_ids=true, to_apply=%region_11.13.clone | all-reduce | flops 8192 | bytes 65536
  511.7 204.4 %all-reduce.8.cloned.1.call-done = f32[32,128,8]{1,2,0:T(8,128)} async-done(((f32[32,128,8]{1,2,0:T(8,128)}), f32[32,128,8]{1,2,0:T(8,128)}) %all-reduce.8.cloned.1.call-update) | async-done | bytes 131088
  716.0 2.6 multiply_convert_fusion
  718.6 39.7 %all_gather.27 = bf16[4096,8]{0,1:T(8,128)(2,1)S(1)} all-gather(bf16[128,8]{0,1:T(8,128)(2,1)S(1)} %get-tuple-element.780), channel_id=1, replica_groups=mesh['row'=8,'col'=32] {'col'}, dimensions={0}, use_global_device_ids=true | all-gather | bytes 67584 | tf_op jit(solution)/shard_map/all_gather | solution.py:166
  758.3 35.1 %all_gather.26 = bf16[1024,8]{0,1:T(8,128)(2,1)S(1)} all-gather(bf16[128,8]{0,1:T(8,128)(2,1)S(1)} %get-tuple-element.780), channel_id=1, replica_groups=mesh['row'=8,'col'=32] {'row'}, dimensions={0}, use_global_device_ids=true | all-gather | bytes 18432 | tf_op jit(solution)/shard_map/all_gather | solution.py:169
  793.4 144.1 %while.33 = (s32[]{:T(128)}, f32[32,128,8]{1,2,0:T(8,128)S(1)}, f32[8,128,8]{1,2,0:T(8,128)S(1)}, s32[]{:T(128)}, s32[256]{0:T(256)}, /*index=5*/bf16[32,128,128...) while((s32[]{:T(128)}, f32[32,128,8]{1,2,0:T(8,128)S(1)}, ...), condition=%wide.region_19.21_spmd.clone.clone, body=%wide.region_14.20_spmd.clone.clone.sunk | while | flops 205513184 | bytes 14005563 | solution.py:102
  796.4 1.9 gather_fusion.11
  812.4 1.9 gather_fusion.11
  828.4 1.9 gather_fusion.11
  844.3 1.9 gather_fusion.11
  860.3 1.9 gather_fusion.11
  876.3 1.9 gather_fusion.11
  892.3 1.9 gather_fusion.11
  908.3 1.9 gather_fusion.11
  924.3 1.9 gather_fusion.11
  938.8 45.4 %all-reduce.3 = f32[8,128,8]{1,2,0:T(8,128)S(1)} all-reduce(f32[8,128,8]{1,2,0:T(8,128)S(1)} %get-tuple-element.393), channel_id=5, replica_groups=mesh['row'=8,'col'=32] {'row'}, use_global_device_ids=true, to_apply=%region_21.23.clone | all-reduce | flops 8192 | bytes 65536
  984.2 204.4 %all-reduce.10.cloned.1.call-done = f32[32,128,8]{1,2,0:T(8,128)} async-done(((f32[32,128,8]{1,2,0:T(8,128)}), f32[32,128,8]{1,2,0:T(8,128)}) %all-reduce.10.cloned.1.call-update) | async-done | bytes 131088
  1188.6 2.2 multiply_reduce_fusion.6
  1190.8 77.3 %all-reduce.4 = (f32[8]{0:T(128)S(1)}, f32[8]{0:T(128)S(1)}, f32[8]{0:T(128)S(1)}) all-reduce(f32[8]{0:T(128)S(1)} %get-tuple-element.680, f32[8]{0:T(128)S(1)} %get-tuple-element.679, f32[8]{0:T(128)S(1)} %get-tuple-element.678), channel_id=1, replica_groups=mesh['row'=8,'col'=32] {'row','col'}, use_global_device_ids=true, to_apply=%region_13.15 | all-reduce | flops 24 | bytes 192 | tf_op jit(solution)/shard_map/psum | solution.py:180
  1268.6 2.7 multiply_subtract_fusion
  (882 shorter events, 265.0 us)
Async XLA Ops:
  7.2 189.1 %all-gather.3.cloned.1.call-start = ((), (), s32[]{:S(2)}) async-start(), calls=%async_computation.1 | async-start | bytes 1081344 | tf_op jit(solution)/shard_map/all_gather | solution.py:139
  9.2 189.0 %all-to-all-start = ((s32[8,1,128]{2,1,0:T(1,128)}), s32[8,1,128]{2,1,0:T(1,128)S(1)}, u32[]{:S(2)}, u32[]{:S(2)}) async-start(s32[8,1,128]{2,1,0:T(1,128)} %stack.2), calls=%async_computation | async-start | bytes 8192 | tf_op jit(solution)/shard_map/all_to_all | solution.py:127
  20.6 695.4 %all-reduce.8.cloned.1.call-start = ((), (), s32[]{:S(2)}) async-start(), calls=%async_computation.2 | async-start | bytes 262144
  201.1 1.9 copy-start.2
  207.5 10.4 copy-start.6
  207.5 10.4 copy-start.8
  221.0 0.7 copy-start.5
  223.8 3.0 copy-start.3
  230.7 1.9 copy-start.2
  237.1 10.4 copy-start.6
  237.1 10.4 copy-start.8
  250.6 0.7 copy-start.5
  253.4 3.0 copy-start.3
  260.3 1.9 copy-start.2
  266.7 10.4 copy-start.6
  266.7 10.4 copy-start.8
  283.0 3.0 copy-start.3
  289.9 1.9 copy-start.2
  296.3 10.4 copy-start.6
  296.3 10.4 copy-start.8
  312.6 3.0 copy-start.3
  319.4 1.9 copy-start.2
  325.9 10.4 copy-start.6
  325.9 10.4 copy-start.8
  339.4 0.7 copy-start.5
  342.2 3.0 copy-start.3
  349.0 1.9 copy-start.2
  355.5 10.4 copy-start.6
  355.5 10.4 copy-start.8
  369.0 0.7 copy-start.5
  371.7 3.0 copy-start.3
  378.6 1.9 copy-start.2
  385.1 10.4 copy-start.6
  385.1 10.4 copy-start.8
  398.6 0.7 copy-start.5
  401.3 3.0 copy-start.3
  408.2 1.9 copy-start.2
  414.7 10.4 copy-start.6
  414.7 10.4 copy-start.8
  428.2 0.7 copy-start.5
  430.9 3.0 copy-start.3
  437.8 1.9 copy-start.2
  444.3 10.4 copy-start.6
  444.3 10.4 copy-start.8
  460.5 3.0 copy-start.3
  465.3 723.3 %all-reduce.10.cloned.1.call-start = ((), (), s32[]{:S(2)}) async-start(), calls=%async_computation.3 | async-start | bytes 262144
  800.4 1.7 copy-start.7
  800.4 1.7 copy-start.9
  816.4 1.7 copy-start.7
  816.4 1.7 copy-start.9
  832.4 1.7 copy-start.7
  832.4 1.7 copy-start.9
  848.4 1.7 copy-start.7
  848.4 1.7 copy-start.9
  864.4 1.7 copy-start.7
  864.4 1.7 copy-start.9
  880.3 1.7 copy-start.7
  880.4 1.7 copy-start.9
  896.3 1.7 copy-start.7
  896.3 1.7 copy-start.9
  912.3 1.7 copy-start.7
  912.3 1.7 copy-start.9
  928.3 1.7 copy-start.7
  928.3 1.7 copy-start.9
  (23 other events, 14.8 us)
Sparse Core Ops, SparseCore 0:
  9.9 63.8 all-gather.2
  465.5 250.5 all-reduce.7
  938.3 250.2 all-reduce.9
